TPU v7x, 256 devices: a whole 4x4x8 slice. The times are simulated.
256 devices in a mesh: gx: 16 (over y_lo, z), gy: 16 (over y_hi, x, core).
Axes of the slice: x: 4, y: 4 (y_hi: 2, y_lo: 2; y = y_hi * 2 + y_lo), z: 8, core: 2. Of those that a mesh axis runs over, the one named last changes fastest.
Arguments:
- obs_values: bfloat16 [4096, 48, 128], P(('gx', 'gy')), may hold values from -1.5 to 1.5
- obs_weight: float32 [4096, 128], P(('gx', 'gy')), may hold values from 0.25 to 4
- obs_box: int32 [4096, 128], P(('gx', 'gy')), may hold values from 0 to 127
- obs_owner: int32 [4096], P(('gx', 'gy')), may hold values from 0 to 255
- block_count: int32 [256], P(('gx', 'gy')), may hold values from 1 to 16, as said below
- diff_x: float32 [48, 128, 2048], P(None, 'gx', 'gy'), may hold values from 0.02 to 0.24
- diff_y: float32 [48, 128, 2048], P(None, 'gx', 'gy'), may hold values from 0.02 to 0.24
- spread_std: float32 [48, 128, 2048], P(None, 'gx', 'gy'), may hold values from 0.3 to 3
- land_sea: int32 [128, 2048], P('gx', 'gy'), may hold values 0 or 1
- vert_corr: float32 [48, 48], replicated, may hold values from -0.12268693 to 1.122687, as said below
Outputs:
- increment: float32 [48, 128, 2048], P(None, 'gx', 'gy')
Inputs may be any that keep to these rules, and one draw needn't show every extreme that they name: `block_count`: some device holds exactly 16 filled blocks in every draw. vert_corr is the identity plus a matrix E whose entries have magnitude at most 0.85 / sqrt(48); it is the same for all columns.
All inputs are finite; a program needn't handle non-finite values. No bound on the sum of `land_sea` on one device may be relied on, other than what follows from the above.
Results may differ from a plain program's by a relative error of at most 0.0003.
Values sent between devices are 32-bit elements; how exact they have to be, the bound alone decides.
A program may use at most 64 MiB of HBM per device.

v0:
```python
import jax
import jax.numpy as jnp
from jax import lax
from jax.sharding import PartitionSpec as P

BOX_DEV = 128
PASSES = 4
HIGH = lax.Precision.HIGHEST


def extended(block, sides, width):
    for axis, dim in sides:
        count = lax.axis_size(axis)
        forward = [(i, i + 1) for i in range(count - 1)]
        forward.append((count - 1, 0))
        backward = [(target, source) for source, target in forward]
        low = lax.ppermute(
            lax.slice_in_dim(block, block.shape[dim] - width, None, axis=dim), axis, forward
        )
        high = lax.ppermute(lax.slice_in_dim(block, 0, width, axis=dim), axis, backward)
        block = jnp.concatenate([low, block, high], axis=dim)
    return block


def one_pass(field, east, north):
    centre = field[:, 1:-1, 1:-1]
    out = centre + east[:, 1:-1, 1:-1] * (field[:, 2:, 1:-1] - centre)
    out = out + east[:, :-2, 1:-1] * (field[:, :-2, 1:-1] - centre)
    out = out + north[:, 1:-1, 1:-1] * (field[:, 1:-1, 2:] - centre)
    out = out + north[:, 1:-1, :-2] * (field[:, 1:-1, :-2] - centre)
    return out


def face_terms(padded, levels):
    diff_east = padded[:levels]
    diff_north = padded[levels : 2 * levels]
    mask = padded[2 * levels]
    east = diff_east[:, :-1, :] * (mask[:-1, :] * mask[1:, :])[None]
    north = diff_north[:, :, :-1] * (mask[:, :-1] * mask[:, 1:])[None]
    east = jnp.pad(east, ((0, 0), (0, 1), (0, 0)))
    north = jnp.pad(north, ((0, 0), (0, 0), (0, 1)))
    return (east, north)


def passes_round(padded, east, north):
    padded = one_pass(padded, east, north)
    return padded


def local(
    obs_values,
    obs_weight,
    obs_box,
    obs_owner,
    block_count,
    diff_x,
    diff_y,
    spread_std,
    land_sea,
    vert_corr,
):
    levels = diff_x.shape[0]
    width_x = diff_x.shape[1]
    width_y = diff_x.shape[2]
    blocks = obs_values.shape[0]
    box_count = BOX_DEV
    filled = (jnp.arange(blocks, dtype=jnp.int32) < block_count[0]).astype(jnp.float32)
    weighted = obs_values.astype(jnp.float32) * (obs_weight * filled[:, None])[:, None, :]
    onehot = (obs_box[:, :, None] == jnp.arange(box_count, dtype=jnp.int32)[None, None, :]).astype(
        jnp.float32
    )
    contrib = jnp.einsum("blo,bok->blk", weighted, onehot, precision=HIGH)
    by_level = lax.all_to_all(contrib, "gy", split_axis=1, concat_axis=0, tiled=True)
    owners = lax.all_gather(obs_owner, "gy", axis=0, tiled=True)
    targets = jnp.arange(lax.axis_size(("gx", "gy")) * 1, dtype=jnp.int32)
    select = (owners[None, :] == targets[:, None]).astype(jnp.float32)
    partial = jnp.einsum("rb,blk->rlk", select, by_level, precision=HIGH)
    mine = lax.psum_scatter(partial, "gx", scatter_dimension=0, tiled=True)
    superob = lax.all_to_all(mine, "gy", split_axis=0, concat_axis=1, tiled=True)[0]
    vbox = jnp.dot(vert_corr, superob, precision=HIGH)
    spread = vbox.reshape(levels, 8, 16)
    spread = jnp.repeat(jnp.repeat(spread, width_x // 8, axis=1), width_y // 16, axis=2)
    mask = land_sea.astype(jnp.float32)
    forcing = spread * spread_std * mask[None]
    depth = 1
    rounds = PASSES // depth
    moved = lax.all_to_all(
        jnp.stack([diff_x, diff_y]), "gy", split_axis=1, concat_axis=3, tiled=True
    )
    mask_whole = lax.all_gather(mask, "gy", axis=1, tiled=True)
    field = lax.all_to_all(forcing, "gy", split_axis=0, concat_axis=2, tiled=True)
    group = field.shape[0]
    stacked = jnp.concatenate([moved[0], moved[1], mask_whole[None]], axis=0)
    stacked = extended(stacked, (("gx", 1),), depth)
    stacked = jnp.pad(stacked, ((0, 0), (0, 0), (depth, depth)))
    east, north = face_terms(stacked, group)
    for turn in range(rounds):
        padded = extended(field, (("gx", 1),), depth)
        padded = jnp.pad(padded, ((0, 0), (0, 0), (depth, depth)))
        field = passes_round(padded, east, north)
    field = lax.all_to_all(field, "gy", split_axis=2, concat_axis=0, tiled=True)
    mixed = jnp.dot(vert_corr, field.reshape(levels, -1), precision=HIGH).reshape(
        levels, width_x, width_y
    )
    return mixed * spread_std * mask[None]


def solution(mesh):
    in_specs = (
        P(("gx", "gy"), None, None),
        P(("gx", "gy"), None),
        P(("gx", "gy"), None),
        P(("gx", "gy")),
        P(("gx", "gy")),
        P(None, "gx", "gy"),
        P(None, "gx", "gy"),
        P(None, "gx", "gy"),
        P("gx", "gy"),
        P(),
    )
    out_specs = P(None, "gx", "gy")
    return jax.shard_map(local, mesh=mesh, in_specs=in_specs, out_specs=out_specs, check_vma=False)
```

profile of v0, /device:TPU:1, one launch (start us, length us, event | category | flops | bytes accessed | tf_op | source)
XLA Modules:
  0.0 235.9 jit_solution(9146900084684502872)
XLA Ops:
  6.5 1.8 pad_maximum_fusion
  8.3 8.4 %all-to-all-start.3 = ((f32[2,48,8,128]{3,2,0,1:T(8,128)}), f32[2,48,8,128]{3,2,0,1:T(8,128)S(1)}, u32[]{:S(2)}, u32[]{:S(2)}) async-start(f32[2,48,8,128]{3,2,0,1:T(8,128)} %pad_maximum_fusion), calls=%async_computation.4 | async-start | bytes 786432 | tf_op jit(solution)/shard_map/all_to_all | solution.py:87
  17.4 0.8 broadcast_multiply_fusion
  18.2 0.7 convert_element_type.28
  18.9 1.7 fusion
  20.6 0.9 copy.48
  21.5 1.3 dynamic-slice
  23.4 0.9 dynamic-update-slice
  24.2 11.3 %all-reduce.5 = s32[256]{0:T(256)S(1)} all-reduce(s32[256]{0:T(256)S(1)} %dynamic-update-slice), channel_id=1, replica_groups=mesh['gx'=16,'gy'=16] {'gy'}, use_global_device_ids=true, to_apply=%add.5 | all-reduce | flops 256 | bytes 2048
  35.5 22.7 %all_gather.7 = f32[8,2048]{1,0:T(8,128)S(1)} all-gather(f32[8,128]{1,0:T(8,128)S(1)} %convert_element_type.28), channel_id=1, replica_groups=mesh['gx'=16,'gy'=16] {'gy'}, dimensions={1}, use_global_device_ids=true | all-gather | bytes 69632 | tf_op jit(solution)/shard_map/all_gather | solution.py:90
  58.3 4.4 %all-to-all-start = ((f32[16,48,128]{2,0,1:T(8,128)}), f32[16,48,128]{2,0,1:T(8,128)S(1)}, u32[]{:S(2)}, u32[]{:S(2)}) async-start(f32[16,48,128]{2,0,1:T(8,128)} %copy.48), calls=%async_computation | async-start | bytes 786432 | tf_op jit(solution)/shard_map/all_to_all | solution.py:73
  63.1 1.7 collective-permute-start
  64.8 4.1 %collective-permute-start.1 = (f32[7,1,2048]{2,1,0:T(1,128)S(1)}, f32[7,1,2048]{2,1,0:T(1,128)S(1)}, u32[]{:S(2)}, u32[]{:S(2)}) collective-permute-start(f32[7,1,2048]{2,1,0:T(1,128)S(1)} %get-tuple-element.6), channel_id=1, source_target_pairs={{16,0},{32,16},{48,32},{64,48},{80,64},{96,80},{112,96},{128,112},... | collective-permute-start | bytes 172040 | tf_op jit(solution)/shard_map/ppermute | solution.py:20
  69.0 3.6 %all-to-all-done = f32[16,48,128]{2,0,1:T(8,128)S(1)} async-done(((f32[16,48,128]{2,0,1:T(8,128)}), f32[16,48,128]{2,0,1:T(8,128)S(1)}, u32[]{:S(2)}, u32[]{:S(2)}) %all-to-all-start) | async-done | bytes 393248 | tf_op jit(solution)/shard_map/all_to_all | solution.py:73
  72.6 1.2 fusion.7
  73.8 0.6 select_maximum_fusion
  74.4 56.3 %reduce-scatter.2.cloned.1.call-done = f32[16,3,128]{2,0,1:T(8,128)} async-done(((f32[256,3,128]{2,0,1:T(8,128)}), f32[16,3,128]{2,0,1:T(8,128)}) %reduce-scatter.2.cloned.1.call-update) | async-done | bytes 24592 | tf_op jit(solution)/shard_map/reduce_scatter | solution.py:78
  130.7 1.4 copy.50
  132.1 19.3 %all-to-all-start.1 = ((f32[16,3,128]{2,1,0:T(4,128)}), f32[16,3,128]{2,1,0:T(4,128)S(1)}, u32[]{:S(2)}, u32[]{:S(2)}) async-start(f32[16,3,128]{2,1,0:T(4,128)} %copy.50), calls=%async_computation.2 | async-start | bytes 65536 | tf_op jit(solution)/shard_map/all_to_all | solution.py:79
  151.3 7.3 %all-to-all-done.1 = f32[16,3,128]{2,1,0:T(4,128)S(1)} async-done(((f32[16,3,128]{2,1,0:T(4,128)}), f32[16,3,128]{2,1,0:T(4,128)S(1)}, u32[]{:S(2)}, u32[]{:S(2)}) %all-to-all-start.1) | async-done | bytes 24608 | tf_op jit(solution)/shard_map/all_to_all | solution.py:79
  159.2 0.7 multiply_multiply_fusion
  159.9 3.7 %all-to-all-start.2 = ((f32[48,8,128]{2,1,0:T(8,128)}), f32[48,8,128]{2,1,0:T(8,128)S(1)}, u32[]{:S(2)}, u32[]{:S(2)}) async-start(f32[48,8,128]{2,1,0:T(8,128)} %multiply_multiply_fusion), calls=%async_computation.3 | async-start | bytes 393216 | tf_op jit(solution)/shard_map/all_to_all | solution.py:91
  163.7 8.1 %all-to-all-done.2 = f32[48,8,128]{2,1,0:T(8,128)S(1)} async-done(((f32[48,8,128]{2,1,0:T(8,128)}), f32[48,8,128]{2,1,0:T(8,128)S(1)}, u32[]{:S(2)}, u32[]{:S(2)}) %all-to-all-start.2) | async-done | bytes 196640 | tf_op jit(solution)/shard_map/all_to_all | solution.py:91
  171.9 0.5 collective-permute-start.2
  172.4 1.0 collective-permute-start.3
  173.5 1.2 collective-permute-done.2
  174.6 2.6 %collective-permute-done.3 = f32[3,1,2048]{2,1,0:T(1,128)S(1)} collective-permute-done((f32[3,1,2048]{2,1,0:T(1,128)S(1)}, f32[3,1,2048]{2,1,0:T(1,128)S(1)}, u32[]{:S(2)}, u32[]{:S(2)}) %collective-permute-start.3) | collective-permute-done | bytes 24608 | tf_op jit(solution)/shard_map/ppermute | solution.py:17
  177.5 0.4 fusion.43
  178.0 1.5 collective-permute-start.5
  179.4 1.2 collective-permute-done.4
  180.6 2.2 collective-permute-done.5
  183.1 0.4 fusion.33
  183.6 1.5 collective-permute-start.7
  185.1 1.2 collective-permute-done.6
  186.3 2.4 %collective-permute-done.7 = f32[3,1,2048]{2,1,0:T(1,128)S(1)} collective-permute-done((f32[3,1,2048]{2,1,0:T(1,128)S(1)}, f32[3,1,2048]{2,1,0:T(1,128)S(1)}, u32[]{:S(2)}, u32[]{:S(2)}) %collective-permute-start.7) | collective-permute-done | bytes 24608 | tf_op jit(solution)/shard_map/ppermute | solution.py:17
  189.0 0.4 fusion.23
  189.5 1.5 collective-permute-start.9
  190.9 1.5 collective-permute-done.8
  192.4 1.9 collective-permute-done.9
  195.0 3.0 %copy.55 = f32[3,8,2048]{1,0,2:T(4,128)} copy(f32[3,8,2048]{2,1,0:T(8,128)S(1)} %fusion.13) | data formatting | bytes 393216 | tf_op jit(solution)/shard_map/add | solution.py:30
  198.0 4.4 %reshape.39 = f32[16,1,3072]{2,1,0:T(1,128)S(1)} reshape(f32[2048,3,8]{2,1,0:T(4,128)} %bitcast.57) | data formatting | bytes 393216
  202.5 16.5 %all_to_all.75 = f32[16,1,3072]{2,1,0:T(1,128)S(1)} all-to-all(f32[16,1,3072]{2,1,0:T(1,128)S(1)} %reshape.39), channel_id=1, replica_groups=mesh['gx'=16,'gy'=16] {'gy'}, dimensions={0} | all-to-all | bytes 393216 | tf_op jit(solution)/shard_map/all_to_all | solution.py:101
  219.0 0.5 broadcast.96
  219.5 1.1 reduce
  220.6 4.1 %reshape.40 = f32[2048,3,8]{2,1,0:T(4,128)} reshape(f32[16,3072]{1,0:T(8,128)S(1)} %reduce) | data formatting | bytes 393216
  224.7 3.3 %copy.56 = f32[3,8,16,128]{3,1,0,2:T(8,128)S(1)} copy(f32[3,8,16,128]{1,0,3,2:T(4,128)} %bitcast.58) | data formatting | bytes 393216 | tf_op jit(solution)/shard_map/all_to_all | solution.py:101
  227.9 0.4 convolution_bitcast_fusion
  228.4 0.7 fusion.9
  (41 shorter events, 3.0 us)
Async XLA Ops:
  6.5 152.1 %copy-start = (f32[48,48]{1,0:T(8,128)S(1)}, f32[48,48]{1,0:T(8,128)}, u32[]{:S(2)}) copy-start(f32[48,48]{1,0:T(8,128)} %param.19) | copy-start | bytes 27652
  8.3 49.9 %all-to-all-start.3 = ((f32[2,48,8,128]{3,2,0,1:T(8,128)}), f32[2,48,8,128]{3,2,0,1:T(8,128)S(1)}, u32[]{:S(2)}, u32[]{:S(2)}) async-start(f32[2,48,8,128]{3,2,0,1:T(8,128)} %pad_maximum_fusion), calls=%async_computation.4 | async-start | bytes 786432 | tf_op jit(solution)/shard_map/all_to_all | solution.py:87
  58.3 14.3 %all-to-all-start = ((f32[16,48,128]{2,0,1:T(8,128)}), f32[16,48,128]{2,0,1:T(8,128)S(1)}, u32[]{:S(2)}, u32[]{:S(2)}) async-start(f32[16,48,128]{2,0,1:T(8,128)} %copy.48), calls=%async_computation | async-start | bytes 786432 | tf_op jit(solution)/shard_map/all_to_all | solution.py:73
  62.7 68.0 %reduce-scatter.2.cloned.1.call-start = ((), (), s32[]{:S(2)}) async-start(), calls=%async_computation.6 | async-start | bytes 417792 | tf_op jit(solution)/shard_map/reduce_scatter | solution.py:78
  62.9 96.3 %copy-start.1 = (f32[48,8,128]{2,1,0:T(8,128)S(1)}, f32[48,8,128]{2,1,0:T(8,128)}, u32[]{:S(2)}) copy-start(f32[48,8,128]{2,1,0:T(8,128)} %param.17) | copy-start | bytes 589828
  63.1 10.7 %collective-permute-start = (f32[7,1,2048]{2,1,0:T(1,128)S(1)}, f32[7,1,2048]{2,1,0:T(1,128)S(1)}, u32[]{:S(2)}, u32[]{:S(2)}) collective-permute-start(f32[7,1,2048]{2,1,0:T(1,128)S(1)} %get-tuple-element.5), channel_id=1, source_target_pairs={{0,16},{16,32},{32,48},{48,64},{64,80},{80,96},{96,112},{112,128},... | collective-permute-start | bytes 172040 | tf_op jit(solution)/shard_map/ppermute | solution.py:17
  64.8 9.0 %collective-permute-start.1 = (f32[7,1,2048]{2,1,0:T(1,128)S(1)}, f32[7,1,2048]{2,1,0:T(1,128)S(1)}, u32[]{:S(2)}, u32[]{:S(2)}) collective-permute-start(f32[7,1,2048]{2,1,0:T(1,128)S(1)} %get-tuple-element.6), channel_id=1, source_target_pairs={{16,0},{32,16},{48,32},{64,48},{80,64},{96,80},{112,96},{128,112},... | collective-permute-start | bytes 172040 | tf_op jit(solution)/shard_map/ppermute | solution.py:20
  132.1 26.6 %all-to-all-start.1 = ((f32[16,3,128]{2,1,0:T(4,128)}), f32[16,3,128]{2,1,0:T(4,128)S(1)}, u32[]{:S(2)}, u32[]{:S(2)}) async-start(f32[16,3,128]{2,1,0:T(4,128)} %copy.50), calls=%async_computation.2 | async-start | bytes 65536 | tf_op jit(solution)/shard_map/all_to_all | solution.py:79
  159.9 11.9 %all-to-all-start.2 = ((f32[48,8,128]{2,1,0:T(8,128)}), f32[48,8,128]{2,1,0:T(8,128)S(1)}, u32[]{:S(2)}, u32[]{:S(2)}) async-start(f32[48,8,128]{2,1,0:T(8,128)} %multiply_multiply_fusion), calls=%async_computation.3 | async-start | bytes 393216 | tf_op jit(solution)/shard_map/all_to_all | solution.py:91
  171.9 2.8 %collective-permute-start.2 = (f32[3,1,2048]{2,1,0:T(1,128)S(1)}, f32[3,1,2048]{2,1,0:T(1,128)S(1)}, u32[]{:S(2)}, u32[]{:S(2)}) collective-permute-start(f32[3,1,2048]{2,1,0:T(1,128)S(1)} %get-tuple-element.16), channel_id=1, source_target_pairs={{16,0},{32,16},{48,32},{64,48},{80,64},{96,80},{112,96},{128,112},... | collective-permute-start | bytes 73736 | tf_op jit(solution)/shard_map/ppermute | solution.py:20
  172.4 4.8 %collective-permute-start.3 = (f32[3,1,2048]{2,1,0:T(1,128)S(1)}, f32[3,1,2048]{2,1,0:T(1,128)S(1)}, u32[]{:S(2)}, u32[]{:S(2)}) collective-permute-start(f32[3,1,2048]{2,1,0:T(1,128)S(1)} %get-tuple-element.15), channel_id=1, source_target_pairs={{0,16},{16,32},{32,48},{48,64},{64,80},{80,96},{96,112},{112,128},... | collective-permute-start | bytes 73736 | tf_op jit(solution)/shard_map/ppermute | solution.py:17
  177.9 2.8 %collective-permute-start.4 = (f32[3,1,2048]{2,1,0:T(1,128)S(1)}, f32[3,1,2048]{2,1,0:T(1,128)S(1)}, u32[]{:S(2)}, u32[]{:S(2)}) collective-permute-start(f32[3,1,2048]{2,1,0:T(1,128)S(1)} %get-tuple-element.14), channel_id=1, source_target_pairs={{16,0},{32,16},{48,32},{64,48},{80,64},{96,80},{112,96},{128,112},... | collective-permute-start | bytes 73736 | tf_op jit(solution)/shard_map/ppermute | solution.py:20
  178.0 4.9 %collective-permute-start.5 = (f32[3,1,2048]{2,1,0:T(1,128)S(1)}, f32[3,1,2048]{2,1,0:T(1,128)S(1)}, u32[]{:S(2)}, u32[]{:S(2)}) collective-permute-start(f32[3,1,2048]{2,1,0:T(1,128)S(1)} %get-tuple-element.13), channel_id=1, source_target_pairs={{0,16},{16,32},{32,48},{48,64},{64,80},{80,96},{96,112},{112,128},... | collective-permute-start | bytes 73736 | tf_op jit(solution)/shard_map/ppermute | solution.py:17
  183.5 2.8 %collective-permute-start.6 = (f32[3,1,2048]{2,1,0:T(1,128)S(1)}, f32[3,1,2048]{2,1,0:T(1,128)S(1)}, u32[]{:S(2)}, u32[]{:S(2)}) collective-permute-start(f32[3,1,2048]{2,1,0:T(1,128)S(1)} %get-tuple-element.12), channel_id=1, source_target_pairs={{16,0},{32,16},{48,32},{64,48},{80,64},{96,80},{112,96},{128,112},... | collective-permute-start | bytes 73736 | tf_op jit(solution)/shard_map/ppermute | solution.py:20
  183.6 5.0 %collective-permute-start.7 = (f32[3,1,2048]{2,1,0:T(1,128)S(1)}, f32[3,1,2048]{2,1,0:T(1,128)S(1)}, u32[]{:S(2)}, u32[]{:S(2)}) collective-permute-start(f32[3,1,2048]{2,1,0:T(1,128)S(1)} %get-tuple-element.11), channel_id=1, source_target_pairs={{0,16},{16,32},{32,48},{48,64},{64,80},{80,96},{96,112},{112,128},... | collective-permute-start | bytes 73736 | tf_op jit(solution)/shard_map/ppermute | solution.py:17
  189.4 3.0 %collective-permute-start.8 = (f32[3,1,2048]{2,1,0:T(1,128)S(1)}, f32[3,1,2048]{2,1,0:T(1,128)S(1)}, u32[]{:S(2)}, u32[]{:S(2)}) collective-permute-start(f32[3,1,2048]{2,1,0:T(1,128)S(1)} %get-tuple-element.10), channel_id=1, source_target_pairs={{16,0},{32,16},{48,32},{64,48},{80,64},{96,80},{112,96},{128,112},... | collective-permute-start | bytes 73736 | tf_op jit(solution)/shard_map/ppermute | solution.py:20
  189.5 4.9 %collective-permute-start.9 = (f32[3,1,2048]{2,1,0:T(1,128)S(1)}, f32[3,1,2048]{2,1,0:T(1,128)S(1)}, u32[]{:S(2)}, u32[]{:S(2)}) collective-permute-start(f32[3,1,2048]{2,1,0:T(1,128)S(1)} %get-tuple-element.9), channel_id=1, source_target_pairs={{0,16},{16,32},{32,48},{48,64},{64,80},{80,96},{96,112},{112,128},... | collective-permute-start | bytes 73736 | tf_op jit(solution)/shard_map/ppermute | solution.py:17
Sparse Core Ops, SparseCore 0:
  73.9 56.7 reduce-scatter.1
where the time goes:
time: 237 us; the launch traced here: 236 us
  waiting for transfers between devices  89.4 us (38%)
  blocking collectives  50.5 us (21%)
  starting transfers between devices  47.9 us (20%)
  local copies, waits for them, and re-layouts  20.5 us (9%)
  between operations  15 us (6%)
  other arithmetic  9.19 us (4%)
  matrix products  3.35 us (1%)
    reduce_scatter x1, waiting for transfers between devices, local(): mine = lax.psum_scatter(partial, 'gx', scatter_dimension=0, tiled=True)  56.3 us
    all_gather x1, blocking collectives, local(): mask_whole = lax.all_gather(mask, 'gy', axis=1, tiled=True)  22.7 us
    all_to_all x1, starting transfers between devices, local(): lax.all_to_all(mine, 'gy', split_axis=0, concat_axis=1, tiled=True)[0]  19.3 us
    all_to_all x1, blocking collectives, local(): field = lax.all_to_all(field, 'gy', split_axis=2, concat_axis=0, tiled=True)  16.5 us
    unnamed x1, blocking collectives  11.3 us
    unnamed x10, local copies, waits for them, and re-layouts  10.7 us
    ppermute x5, waiting for transfers between devices, extended(): lax.ppermute(lax.slice_in_dim(block, block.shape[dim] - width, None, axis...  9.05 us
    all_to_all x1, starting transfers between devices, local(): lax.all_to_all(jnp.stack([diff_x, diff_y]), 'gy', split_axis=1, concat_ax...  8.45 us
  transfers between devices with their start and end apart: 15, of which 12 were waited for; matrix products, arithmetic and copies ran while one was open for 4% of the time, Pallas kernels for 0%

commit v1 on v0

--- a/solution.py
+++ b/solution.py
@@ -87,7 +87,8 @@
     moved = lax.all_to_all(
         jnp.stack([diff_x, diff_y]), "gy", split_axis=1, concat_axis=3, tiled=True
     )
-    mask_whole = lax.all_gather(mask, "gy", axis=1, tiled=True)
+    outgoing = jnp.stack([mask] * lax.axis_size("gy"))
+    mask_whole = jnp.concatenate(lax.all_to_all(outgoing, "gy", 0, 0), axis=1)
     field = lax.all_to_all(forcing, "gy", split_axis=0, concat_axis=2, tiled=True)
     group = field.shape[0]
     stacked = jnp.concatenate([moved[0], moved[1], mask_whole[None]], axis=0)

time: 237 us -> 229 us (0.966)
  blocking collectives: 50.5 us -> 27.9 us
  waiting for transfers between devices: 89.4 us -> 97.6 us
  starting transfers between devices: 47.9 us -> 53.8 us
    all_gather x1 -> x0, blocking collectives: 22.7 us -> none  [local(): mask_whole = lax.all_gather(mask, 'gy', axis=1, tiled=True)]
    all_to_all x1, waiting for transfers between devices: 0.01 us -> 7.66 us  [local(): lax.all_to_all(jnp.stack([diff_x, diff_y]), 'gy', split_axis=1, concat_ax...]
    all_to_all x0 -> x1, starting transfers between devices: none -> 4.33 us  [local(): mask_whole = jnp.concatenate(lax.all_to_all(outgoing, 'gy', 0, 0), axis=1)]
  transfers between devices with their start and end apart: 15 -> 16, of which waited for: 12 -> 13; matrix products, arithmetic and copies ran while one was open for 4% -> 4% of each run, Pallas kernels for 0% -> 0%
where the time goes in v1:
time: 229 us; the launch traced here: 228 us
  waiting for transfers between devices  97.6 us (43%)
  starting transfers between devices  53.8 us (23%)
  blocking collectives  27.9 us (12%)
  local copies, waits for them, and re-layouts  21.1 us (9%)
  between operations  14.9 us (7%)
  other arithmetic  9.2 us (4%)
  matrix products  3.35 us (1%)
    reduce_scatter x1, waiting for transfers between devices, local(): mine = lax.psum_scatter(partial, 'gx', scatter_dimension=0, tiled=True)  56.4 us
    all_to_all x1, starting transfers between devices, local(): lax.all_to_all(mine, 'gy', split_axis=0, concat_axis=1, tiled=True)[0]  19 us
    all_to_all x1, blocking collectives, local(): field = lax.all_to_all(field, 'gy', split_axis=2, concat_axis=0, tiled=True)  16.5 us
    unnamed x1, blocking collectives  11.4 us
    unnamed x10, local copies, waits for them, and re-layouts  10.6 us
    ppermute x5, waiting for transfers between devices, extended(): lax.ppermute(lax.slice_in_dim(block, block.shape[dim] - width, None, axis...  9.09 us
    all_to_all x1, starting transfers between devices, local(): lax.all_to_all(jnp.stack([diff_x, diff_y]), 'gy', split_axis=1, concat_ax...  8.45 us
    all_to_all x1, waiting for transfers between devices, local(): lax.all_to_all(forcing, 'gy', split_axis=0, concat_axis=2, tiled=True)  8.12 us
  transfers between devices with their start and end apart: 16, of which 13 were waited for; matrix products, arithmetic and copies ran while one was open for 4% of the time, Pallas kernels for 0%

profile of v1, /device:TPU:1, one launch (start us, length us, event | category | flops | bytes accessed | tf_op | source)
XLA Modules:
  0.0 227.9 jit_solution(3294439130420318315)
XLA Ops:
  6.5 1.8 pad_maximum_fusion
  8.3 8.4 %all-to-all-start.3 = ((f32[2,48,8,128]{3,2,0,1:T(8,128)}), f32[2,48,8,128]{3,2,0,1:T(8,128)S(1)}, u32[]{:S(2)}, u32[]{:S(2)}) async-start(f32[2,48,8,128]{3,2,0,1:T(8,128)} %pad_maximum_fusion), calls=%async_computation.4 | async-start | bytes 786432 | tf_op jit(solution)/shard_map/all_to_all | solution.py:87
  16.8 0.7 convert_element_type.28
  18.1 0.8 broadcast_multiply_fusion
  18.9 7.7 %all-to-all-done.3 = f32[2,48,8,128]{3,2,0,1:T(8,128)S(1)} async-done(((f32[2,48,8,128]{3,2,0,1:T(8,128)}), f32[2,48,8,128]{3,2,0,1:T(8,128)S(1)}, u32[]{:S(2)}, u32[]{:S(2)}) %all-to-all-start.3) | async-done | bytes 393248 | tf_op jit(solution)/shard_map/all_to_all | solution.py:87
  26.6 0.6 stack.11
  27.2 4.3 %all-to-all-start.4 = ((f32[16,8,128]{2,1,0:T(8,128)}), f32[16,8,128]{2,1,0:T(8,128)S(1)}, u32[]{:S(2)}, u32[]{:S(2)}) async-start(f32[16,8,128]{2,1,0:T(8,128)} %stack.11), calls=%async_computation.5 | async-start | bytes 131072 | tf_op jit(solution)/shard_map/all_to_all | solution.py:91
  31.5 1.7 fusion
  33.2 0.9 copy.48
  34.1 1.2 dynamic-slice
  35.9 0.9 dynamic-update-slice
  36.7 11.4 %all-reduce.5 = s32[256]{0:T(256)S(1)} all-reduce(s32[256]{0:T(256)S(1)} %dynamic-update-slice), channel_id=1, replica_groups=mesh['gx'=16,'gy'=16] {'gy'}, use_global_device_ids=true, to_apply=%add.5 | all-reduce | flops 256 | bytes 2048
  48.3 6.3 %all-to-all-start = ((f32[16,48,128]{2,0,1:T(8,128)}), f32[16,48,128]{2,0,1:T(8,128)S(1)}, u32[]{:S(2)}, u32[]{:S(2)}) async-start(f32[16,48,128]{2,0,1:T(8,128)} %copy.48), calls=%async_computation | async-start | bytes 786432 | tf_op jit(solution)/shard_map/all_to_all | solution.py:73
  54.8 1.7 collective-permute-start
  56.6 4.1 %collective-permute-start.1 = (f32[7,1,2048]{2,1,0:T(1,128)S(1)}, f32[7,1,2048]{2,1,0:T(1,128)S(1)}, u32[]{:S(2)}, u32[]{:S(2)}) collective-permute-start(f32[7,1,2048]{2,1,0:T(1,128)S(1)} %get-tuple-element.6), channel_id=1, source_target_pairs={{16,0},{32,16},{48,32},{64,48},{80,64},{96,80},{112,96},{128,112},... | collective-permute-start | bytes 172040 | tf_op jit(solution)/shard_map/ppermute | solution.py:20
  60.7 3.9 %all-to-all-done = f32[16,48,128]{2,0,1:T(8,128)S(1)} async-done(((f32[16,48,128]{2,0,1:T(8,128)}), f32[16,48,128]{2,0,1:T(8,128)S(1)}, u32[]{:S(2)}, u32[]{:S(2)}) %all-to-all-start) | async-done | bytes 393248 | tf_op jit(solution)/shard_map/all_to_all | solution.py:73
  64.6 1.2 fusion.7
  65.9 0.6 select_maximum_fusion
  66.5 56.4 %reduce-scatter.2.cloned.1.call-done = f32[16,3,128]{2,0,1:T(8,128)} async-done(((f32[256,3,128]{2,0,1:T(8,128)}), f32[16,3,128]{2,0,1:T(8,128)}) %reduce-scatter.2.cloned.1.call-update) | async-done | bytes 24592 | tf_op jit(solution)/shard_map/reduce_scatter | solution.py:78
  123.0 1.4 copy.50
  124.3 19.0 %all-to-all-start.1 = ((f32[16,3,128]{2,1,0:T(4,128)}), f32[16,3,128]{2,1,0:T(4,128)S(1)}, u32[]{:S(2)}, u32[]{:S(2)}) async-start(f32[16,3,128]{2,1,0:T(4,128)} %copy.50), calls=%async_computation.2 | async-start | bytes 65536 | tf_op jit(solution)/shard_map/all_to_all | solution.py:79
  143.3 7.3 %all-to-all-done.1 = f32[16,3,128]{2,1,0:T(4,128)S(1)} async-done(((f32[16,3,128]{2,1,0:T(4,128)}), f32[16,3,128]{2,1,0:T(4,128)S(1)}, u32[]{:S(2)}, u32[]{:S(2)}) %all-to-all-start.1) | async-done | bytes 24608 | tf_op jit(solution)/shard_map/all_to_all | solution.py:79
  151.1 0.7 multiply_multiply_fusion
  151.8 3.7 %all-to-all-start.2 = ((f32[48,8,128]{2,1,0:T(8,128)}), f32[48,8,128]{2,1,0:T(8,128)S(1)}, u32[]{:S(2)}, u32[]{:S(2)}) async-start(f32[48,8,128]{2,1,0:T(8,128)} %multiply_multiply_fusion), calls=%async_computation.3 | async-start | bytes 393216 | tf_op jit(solution)/shard_map/all_to_all | solution.py:92
  155.7 8.1 %all-to-all-done.2 = f32[48,8,128]{2,1,0:T(8,128)S(1)} async-done(((f32[48,8,128]{2,1,0:T(8,128)}), f32[48,8,128]{2,1,0:T(8,128)S(1)}, u32[]{:S(2)}, u32[]{:S(2)}) %all-to-all-start.2) | async-done | bytes 196640 | tf_op jit(solution)/shard_map/all_to_all | solution.py:92
  163.8 0.6 collective-permute-start.2
  164.4 1.0 collective-permute-start.3
  165.4 1.2 collective-permute-done.2
  166.6 2.6 %collective-permute-done.3 = f32[3,1,2048]{2,1,0:T(1,128)S(1)} collective-permute-done((f32[3,1,2048]{2,1,0:T(1,128)S(1)}, f32[3,1,2048]{2,1,0:T(1,128)S(1)}, u32[]{:S(2)}, u32[]{:S(2)}) %collective-permute-start.3) | collective-permute-done | bytes 24608 | tf_op jit(solution)/shard_map/ppermute | solution.py:17
  169.5 0.4 fusion.43
  170.0 1.5 collective-permute-start.5
  171.4 1.2 collective-permute-done.4
  172.7 2.2 collective-permute-done.5
  175.6 1.5 collective-permute-start.7
  177.1 1.2 collective-permute-done.6
  178.3 2.4 %collective-permute-done.7 = f32[3,1,2048]{2,1,0:T(1,128)S(1)} collective-permute-done((f32[3,1,2048]{2,1,0:T(1,128)S(1)}, f32[3,1,2048]{2,1,0:T(1,128)S(1)}, u32[]{:S(2)}, u32[]{:S(2)}) %collective-permute-start.7) | collective-permute-done | bytes 24608 | tf_op jit(solution)/shard_map/ppermute | solution.py:17
  181.5 1.5 collective-permute-start.9
  182.9 1.5 collective-permute-done.8
  184.4 1.9 collective-permute-done.9
  187.0 3.0 %copy.55 = f32[3,8,2048]{1,0,2:T(4,128)} copy(f32[3,8,2048]{2,1,0:T(8,128)S(1)} %fusion.13) | data formatting | bytes 393216 | tf_op jit(solution)/shard_map/add | solution.py:30
  190.0 4.4 %reshape.45 = f32[16,1,3072]{2,1,0:T(1,128)S(1)} reshape(f32[2048,3,8]{2,1,0:T(4,128)} %bitcast.59) | data formatting | bytes 393216
  194.5 16.5 %all_to_all.80 = f32[16,1,3072]{2,1,0:T(1,128)S(1)} all-to-all(f32[16,1,3072]{2,1,0:T(1,128)S(1)} %reshape.45), channel_id=1, replica_groups=mesh['gx'=16,'gy'=16] {'gy'}, dimensions={0} | all-to-all | bytes 393216 | tf_op jit(solution)/shard_map/all_to_all | solution.py:102
  211.0 0.5 broadcast.98
  211.5 1.1 reduce
  212.6 4.0 %reshape.46 = f32[2048,3,8]{2,1,0:T(4,128)} reshape(f32[16,3072]{1,0:T(8,128)S(1)} %reduce) | data formatting | bytes 393216
  216.6 3.3 %copy.56 = f32[3,8,16,128]{3,1,0,2:T(8,128)S(1)} copy(f32[3,8,16,128]{1,0,3,2:T(4,128)} %bitcast.60) | data formatting | bytes 393216 | tf_op jit(solution)/shard_map/all_to_all | solution.py:102
  219.9 0.4 convolution_bitcast_fusion
  220.4 0.7 fusion.9
  (43 shorter events, 3.7 us)
Async XLA Ops:
  6.5 144.1 %copy-start = (f32[48,48]{1,0:T(8,128)S(1)}, f32[48,48]{1,0:T(8,128)}, u32[]{:S(2)}) copy-start(f32[48,48]{1,0:T(8,128)} %param.19) | copy-start | bytes 27652
  8.3 18.2 %all-to-all-start.3 = ((f32[2,48,8,128]{3,2,0,1:T(8,128)}), f32[2,48,8,128]{3,2,0,1:T(8,128)S(1)}, u32[]{:S(2)}, u32[]{:S(2)}) async-start(f32[2,48,8,128]{3,2,0,1:T(8,128)} %pad_maximum_fusion), calls=%async_computation.4 | async-start | bytes 786432 | tf_op jit(solution)/shard_map/all_to_all | solution.py:87
  27.2 21.0 %all-to-all-start.4 = ((f32[16,8,128]{2,1,0:T(8,128)}), f32[16,8,128]{2,1,0:T(8,128)S(1)}, u32[]{:S(2)}, u32[]{:S(2)}) async-start(f32[16,8,128]{2,1,0:T(8,128)} %stack.11), calls=%async_computation.5 | async-start | bytes 131072 | tf_op jit(solution)/shard_map/all_to_all | solution.py:91
  48.3 16.3 %all-to-all-start = ((f32[16,48,128]{2,0,1:T(8,128)}), f32[16,48,128]{2,0,1:T(8,128)S(1)}, u32[]{:S(2)}, u32[]{:S(2)}) async-start(f32[16,48,128]{2,0,1:T(8,128)} %copy.48), calls=%async_computation | async-start | bytes 786432 | tf_op jit(solution)/shard_map/all_to_all | solution.py:73
  54.6 68.4 %reduce-scatter.2.cloned.1.call-start = ((), (), s32[]{:S(2)}) async-start(), calls=%async_computation.7 | async-start | bytes 417792 | tf_op jit(solution)/shard_map/reduce_scatter | solution.py:78
  54.7 96.5 %copy-start.1 = (f32[48,8,128]{2,1,0:T(8,128)S(1)}, f32[48,8,128]{2,1,0:T(8,128)}, u32[]{:S(2)}) copy-start(f32[48,8,128]{2,1,0:T(8,128)} %param.17) | copy-start | bytes 589828
  54.8 11.0 %collective-permute-start = (f32[7,1,2048]{2,1,0:T(1,128)S(1)}, f32[7,1,2048]{2,1,0:T(1,128)S(1)}, u32[]{:S(2)}, u32[]{:S(2)}) collective-permute-start(f32[7,1,2048]{2,1,0:T(1,128)S(1)} %get-tuple-element.5), channel_id=1, source_target_pairs={{0,16},{16,32},{32,48},{48,64},{64,80},{80,96},{96,112},{112,128},... | collective-permute-start | bytes 172040 | tf_op jit(solution)/shard_map/ppermute | solution.py:17
  56.6 9.3 %collective-permute-start.1 = (f32[7,1,2048]{2,1,0:T(1,128)S(1)}, f32[7,1,2048]{2,1,0:T(1,128)S(1)}, u32[]{:S(2)}, u32[]{:S(2)}) collective-permute-start(f32[7,1,2048]{2,1,0:T(1,128)S(1)} %get-tuple-element.6), channel_id=1, source_target_pairs={{16,0},{32,16},{48,32},{64,48},{80,64},{96,80},{112,96},{128,112},... | collective-permute-start | bytes 172040 | tf_op jit(solution)/shard_map/ppermute | solution.py:20
  124.3 26.3 %all-to-all-start.1 = ((f32[16,3,128]{2,1,0:T(4,128)}), f32[16,3,128]{2,1,0:T(4,128)S(1)}, u32[]{:S(2)}, u32[]{:S(2)}) async-start(f32[16,3,128]{2,1,0:T(4,128)} %copy.50), calls=%async_computation.2 | async-start | bytes 65536 | tf_op jit(solution)/shard_map/all_to_all | solution.py:79
  151.8 11.9 %all-to-all-start.2 = ((f32[48,8,128]{2,1,0:T(8,128)}), f32[48,8,128]{2,1,0:T(8,128)S(1)}, u32[]{:S(2)}, u32[]{:S(2)}) async-start(f32[48,8,128]{2,1,0:T(8,128)} %multiply_multiply_fusion), calls=%async_computation.3 | async-start | bytes 393216 | tf_op jit(solution)/shard_map/all_to_all | solution.py:92
  163.8 2.8 %collective-permute-start.2 = (f32[3,1,2048]{2,1,0:T(1,128)S(1)}, f32[3,1,2048]{2,1,0:T(1,128)S(1)}, u32[]{:S(2)}, u32[]{:S(2)}) collective-permute-start(f32[3,1,2048]{2,1,0:T(1,128)S(1)} %get-tuple-element.16), channel_id=1, source_target_pairs={{16,0},{32,16},{48,32},{64,48},{80,64},{96,80},{112,96},{128,112},... | collective-permute-start | bytes 73736 | tf_op jit(solution)/shard_map/ppermute | solution.py:20
  164.4 4.8 %collective-permute-start.3 = (f32[3,1,2048]{2,1,0:T(1,128)S(1)}, f32[3,1,2048]{2,1,0:T(1,128)S(1)}, u32[]{:S(2)}, u32[]{:S(2)}) collective-permute-start(f32[3,1,2048]{2,1,0:T(1,128)S(1)} %get-tuple-element.15), channel_id=1, source_target_pairs={{0,16},{16,32},{32,48},{48,64},{64,80},{80,96},{96,112},{112,128},... | collective-permute-start | bytes 73736 | tf_op jit(solution)/shard_map/ppermute | solution.py:17
  169.9 2.8 %collective-permute-start.4 = (f32[3,1,2048]{2,1,0:T(1,128)S(1)}, f32[3,1,2048]{2,1,0:T(1,128)S(1)}, u32[]{:S(2)}, u32[]{:S(2)}) collective-permute-start(f32[3,1,2048]{2,1,0:T(1,128)S(1)} %get-tuple-element.14), channel_id=1, source_target_pairs={{16,0},{32,16},{48,32},{64,48},{80,64},{96,80},{112,96},{128,112},... | collective-permute-start | bytes 73736 | tf_op jit(solution)/shard_map/ppermute | solution.py:20
  170.0 4.9 %collective-permute-start.5 = (f32[3,1,2048]{2,1,0:T(1,128)S(1)}, f32[3,1,2048]{2,1,0:T(1,128)S(1)}, u32[]{:S(2)}, u32[]{:S(2)}) collective-permute-start(f32[3,1,2048]{2,1,0:T(1,128)S(1)} %get-tuple-element.13), channel_id=1, source_target_pairs={{0,16},{16,32},{32,48},{48,64},{64,80},{80,96},{96,112},{112,128},... | collective-permute-start | bytes 73736 | tf_op jit(solution)/shard_map/ppermute | solution.py:17
  175.5 2.8 %collective-permute-start.6 = (f32[3,1,2048]{2,1,0:T(1,128)S(1)}, f32[3,1,2048]{2,1,0:T(1,128)S(1)}, u32[]{:S(2)}, u32[]{:S(2)}) collective-permute-start(f32[3,1,2048]{2,1,0:T(1,128)S(1)} %get-tuple-element.12), channel_id=1, source_target_pairs={{16,0},{32,16},{48,32},{64,48},{80,64},{96,80},{112,96},{128,112},... | collective-permute-start | bytes 73736 | tf_op jit(solution)/shard_map/ppermute | solution.py:20
  175.6 5.0 %collective-permute-start.7 = (f32[3,1,2048]{2,1,0:T(1,128)S(1)}, f32[3,1,2048]{2,1,0:T(1,128)S(1)}, u32[]{:S(2)}, u32[]{:S(2)}) collective-permute-start(f32[3,1,2048]{2,1,0:T(1,128)S(1)} %get-tuple-element.11), channel_id=1, source_target_pairs={{0,16},{16,32},{32,48},{48,64},{64,80},{80,96},{96,112},{112,128},... | collective-permute-start | bytes 73736 | tf_op jit(solution)/shard_map/ppermute | solution.py:17
  181.4 3.0 %collective-permute-start.8 = (f32[3,1,2048]{2,1,0:T(1,128)S(1)}, f32[3,1,2048]{2,1,0:T(1,128)S(1)}, u32[]{:S(2)}, u32[]{:S(2)}) collective-permute-start(f32[3,1,2048]{2,1,0:T(1,128)S(1)} %get-tuple-element.10), channel_id=1, source_target_pairs={{16,0},{32,16},{48,32},{64,48},{80,64},{96,80},{112,96},{128,112},... | collective-permute-start | bytes 73736 | tf_op jit(solution)/shard_map/ppermute | solution.py:20
  181.5 4.9 %collective-permute-start.9 = (f32[3,1,2048]{2,1,0:T(1,128)S(1)}, f32[3,1,2048]{2,1,0:T(1,128)S(1)}, u32[]{:S(2)}, u32[]{:S(2)}) collective-permute-start(f32[3,1,2048]{2,1,0:T(1,128)S(1)} %get-tuple-element.9), channel_id=1, source_target_pairs={{0,16},{16,32},{32,48},{48,64},{64,80},{80,96},{96,112},{112,128},... | collective-permute-start | bytes 73736 | tf_op jit(solution)/shard_map/ppermute | solution.py:17
Sparse Core Ops, SparseCore 0:
  66.0 56.9 reduce-scatter.1
